TPU v7x, 768 devices: a whole 4x8x12 slice. The times are simulated.
768 devices in a mesh: energy: 32 (over y, x), slab: 24 (over z, core).
Axes of the slice: x: 4, y: 8, z: 12, core: 2. Of those that a mesh axis runs over, the one named last changes fastest.
Arguments:
- g_lesser: bfloat16 [32, 24, 320, 640], P('energy', 'slab'), may hold values from -6 to 6
- g_retarded: bfloat16 [32, 24, 320, 640], P('energy', 'slab'), may hold values from -0.25 to 0.25
- screened: bfloat16 [32, 24, 320, 640], P(None, 'slab', 'energy'), may hold values from -1 to 1
- coupling: bfloat16 [24, 320, 320], P('slab'), may hold values from -1.5 to 1.5, as said below
Outputs:
- correction: bfloat16 [32, 24, 320, 640], P('energy', 'slab')
Inputs may be any that keep to these rules, and one draw needn't show every extreme that they name: `coupling`: coupling_s is the diagonal entries between 0.75 and 1 plus independent small entries.
All inputs are finite; a program needn't handle non-finite values.
Results may differ from a plain program's by a relative error of at most 0.02.
Values may be sent and summed in bfloat16 or wider, within the bound.
A program may use at most 64 MiB of HBM per device.

v0:
```python
import math

import jax
import jax.numpy as jnp
from jax import lax
from jax.sharding import PartitionSpec as P


def entering(part, axis, combine, identity):
    place = lax.axis_index(axis)
    gathered = jax.tree.map(lambda a: lax.all_gather(a, axis), part)
    state = jax.tree.map(lambda a, e: jnp.zeros_like(a) + jnp.asarray(e, a.dtype), part, identity)

    def one(lap, state):
        return combine(
            state, jax.tree.map(lambda a: lax.dynamic_index_in_dim(a, lap, 0, False), gathered)
        )

    return lax.fori_loop(0, place, one, state)


def spectral(owned, inter):
    count = owned.shape[0]
    half = owned.shape[-1] // 2
    rows = owned.shape[2]
    length = 2 * count
    freq = jnp.arange(length, dtype=jnp.int32)[:, None]
    point = jnp.arange(count, dtype=jnp.int32)[None, :]
    phase = (freq * point % length).astype(jnp.float32) * (2.0 * math.pi / length)
    fwd_re = jnp.cos(phase)
    fwd_im = -jnp.sin(phase)
    inv_re = jnp.cos(phase).T / length
    inv_im = jnp.sin(phase).T / length
    exact = lax.Precision.HIGHEST

    def forward(block):
        values = block.astype(jnp.float32)
        part_re = values[..., :half].reshape(count, -1)
        part_im = values[..., half:].reshape(count, -1)
        out_re = jnp.dot(fwd_re, part_re, precision=exact) - jnp.dot(
            fwd_im, part_im, precision=exact
        )
        out_im = jnp.dot(fwd_re, part_im, precision=exact) + jnp.dot(
            fwd_im, part_re, precision=exact
        )
        return (out_re, out_im)

    lesser_re, lesser_im = forward(owned)
    inter_re, inter_im = forward(inter)
    prod_re = lesser_re * inter_re - lesser_im * inter_im
    prod_im = lesser_re * inter_im + lesser_im * inter_re
    conv_re = jnp.dot(inv_re, prod_re, precision=exact) - jnp.dot(inv_im, prod_im, precision=exact)
    conv_im = jnp.dot(inv_re, prod_im, precision=exact) + jnp.dot(inv_im, prod_re, precision=exact)
    shape = (count, owned.shape[1], rows, half)
    return jnp.concatenate([-conv_im.reshape(shape), conv_re.reshape(shape)], axis=-1).astype(
        jnp.bfloat16
    )


def transport(link, state):
    count = state.shape[0]
    half = state.shape[-1] // 2
    left = jnp.einsum("ab,nbc->nac", link, state, preferred_element_type=jnp.float32).astype(
        jnp.bfloat16
    )
    parts = left.reshape(count, half, 2, half)
    moved = jnp.einsum("nakb,cb->nakc", parts, link, preferred_element_type=jnp.float32)
    return moved.reshape(count, half, 2 * half)


def sandwich(green, state):
    half = green.shape[-1] // 2
    green_re = green[..., :half]
    green_im = green[..., half:]
    state_re = state[..., :half]
    state_im = state[..., half:]
    right_mat = jnp.concatenate(
        [jnp.concatenate([state_re, state_im], -1), jnp.concatenate([-state_im, state_re], -1)], 1
    )
    left = jnp.einsum("nab,nbc->nac", green, right_mat, preferred_element_type=jnp.float32).astype(
        jnp.bfloat16
    )
    tr_re = jnp.swapaxes(green_re, 1, 2)
    tr_im = jnp.swapaxes(green_im, 1, 2)
    adjoint = jnp.concatenate(
        [jnp.concatenate([tr_re, -tr_im], -1), jnp.concatenate([tr_im, tr_re], -1)], 1
    )
    return jnp.einsum("nab,nbc->nac", left, adjoint, preferred_element_type=jnp.float32).astype(
        jnp.bfloat16
    )


def compose(earlier, later):
    link_one, state_one = earlier
    link_two, state_two = later
    joined = jnp.dot(link_two, link_one, preferred_element_type=jnp.float32).astype(jnp.bfloat16)
    carried = (transport(link_two, state_one) + state_two.astype(jnp.float32)).astype(jnp.bfloat16)
    return (joined, carried)


def local(g_lesser, g_retarded, screened, coupling):
    owned = lax.all_to_all(g_lesser, "energy", split_axis=2, concat_axis=0, tiled=True)
    sigma_rows = spectral(owned, screened)
    sigma = lax.all_to_all(sigma_rows, "energy", split_axis=0, concat_axis=2, tiled=True)[:, 0]
    link = coupling[0]
    green = g_retarded[:, 0]
    identity = (jnp.eye(link.shape[0], dtype=jnp.bfloat16), jnp.zeros_like(sigma))
    prior_link, prior_state = entering((link, sigma), "slab", compose, identity)
    state = sigma.astype(jnp.float32) + transport(link, prior_state)
    return sandwich(green, state.astype(jnp.bfloat16))[:, None]


def solution(mesh):
    placed = (
        P("energy", "slab", None, None),
        P("energy", "slab", None, None),
        P(None, "slab", "energy", None),
        P("slab", None, None),
    )
    return jax.shard_map(
        local,
        mesh=mesh,
        in_specs=placed,
        out_specs=P("energy", "slab", None, None),
        check_vma=False,
    )
```

profile of v0, /device:TPU:705, one launch (start us, length us, event | category | flops | bytes accessed | tf_op | source)
XLA Modules:
  0.0 273.7 jit_solution(14696486908138712436)
XLA Ops:
  7.3 1.6 copy.42
  9.4 3.1 %reduce.2 = bf16[320,640]{1,0:T(8,128)(2,1)S(1)} reduce(bf16[320,1,1,640]{3,2,1,0:T(2,128)(2,1)S(1)} %bitcast.94, bf16[]{:T(256)} %broadcast.79), dimensions={1,2}, to_apply=%bitcast.80.reduce_sub_computation | reduce | bytes 819202
  13.5 9.8 %all-to-all-start = ((bf16[32,2,3200]{2,1,0:T(2,128)(2,1)}), bf16[32,2,3200]{2,1,0:T(2,128)(2,1)}, u32[]{:S(2)}, u32[]{:S(2)}) async-start(bf16[32,2,3200]{2,1,0:T(2,128)(2,1)} %reshape.188), calls=%async_computation | async-start | bytes 819200 | tf_op jit(solution)/shard_map/all_to_all | solution.py:102
  26.5 10.7 %all-to-all-done = bf16[32,2,3200]{2,1,0:T(2,128)(2,1)} async-done(((bf16[32,2,3200]{2,1,0:T(2,128)(2,1)}), bf16[32,2,3200]{2,1,0:T(2,128)(2,1)}, u32[]{:S(2)}, u32[]{:S(2)}) %all-to-all-start) | async-done | bytes 409632 | tf_op jit(solution)/shard_map/all_to_all | solution.py:102
  37.2 2.8 %reshape.189 = bf16[320,1,1,640]{3,2,1,0:T(2,128)(2,1)S(1)} reshape(bf16[32,2,3200]{2,1,0:T(2,128)(2,1)} %all-to-all-done) | data formatting | bytes 819200
  40.0 2.4 bitcast_reduce_fusion
  49.1 22.9 %all_to_all.24 = bf16[32,1,10,640]{3,2,1,0:T(8,128)(2,1)S(1)} all-to-all(bf16[32,1,10,640]{3,2,1,0:T(8,128)(2,1)S(1)} %maximum_bitcast_fusion.2), channel_id=1, replica_groups=mesh['energy'=32,'slab'=24] {'energy'}, dimensions={0} | all-to-all | bytes 819200 | tf_op jit(solution)/shard_map/all_to_all | solution.py:104
  75.5 66.2 %all-gather.5.cloned.1.call-done = bf16[24,1,320,640]{3,2,1,0:T(8,128)(2,1)} async-done(((bf16[1,1,320,640]{3,2,1,0:T(8,128)(2,1)}), bf16[24,1,320,640]{3,2,1,0:T(8,128)(2,1)}) %all-gather.5.cloned.1.call-update) | async-done | bytes 9830416 | tf_op jit(solution)/shard_map/all_gather | solution.py:11
  141.8 106.7 %while.12 = (s32[]{:T(128)}, bf16[1,320,640]{1,2,0:T(8,128)(2,1)S(1)}, s32[]{:T(128)}, bf16[24,320,320]{2,1,0:T(8,128)(2,1)}, bf16[24,1,320,640]{3,2,1,0:T(8,128)(2,1)}, /*index=5*/s32[]{:T(128)}, s32[]{:T(128)}, s32[]{:T(128)}) while((s32[]{:T(128)}, bf16[1,320,640]{1,2,0:T(8,128)(2,1)S(1)}, s32[]{:T(128)}, bf16[24,320,320]{2,1,0:T(8,128)(2,1)}, ...), condition=%wide.region_1.2_spmd, body=%wide.region_0.1_spmd.sunk | while | flops 262963200 | bytes 6635651 | solution.py:19
  141.9 1.4 fusion.147
  143.7 1.4 fusion.148
  148.3 1.4 fusion.148
  152.9 1.4 fusion.148
  157.6 1.4 fusion.148
  162.2 1.4 fusion.148
  166.8 1.4 fusion.148
  171.5 1.4 fusion.148
  176.1 1.4 fusion.148
  180.7 1.4 fusion.148
  185.3 1.4 fusion.148
  190.0 1.4 fusion.148
  194.6 1.4 fusion.148
  199.2 1.4 fusion.148
  203.8 1.4 fusion.148
  208.5 1.4 fusion.148
  217.7 1.4 fusion.148
  222.3 1.4 fusion.148
  231.6 1.4 fusion.148
  236.2 1.4 fusion.148
  245.5 1.4 fusion.148
  252.8 12.3 %maximum_maximum_fusion = bf16[1,640,640]{2,0,1:T(2,128)(2,1)S(1)} fusion(bf16[1,320,320]{2,0,1:T(2,128)(2,1)S(1)} %get-tuple-element.78, bf16[1,320,320]{2,0,1:T(2,128)(2,1)S(1)} %get-tuple-element.77, bf16[1,320,640]{2,0,1:T(2,128)(2,1)S(1)} %add_convert_fusion), kind=kLoop, calls=%fused_computation.23 | loop fusion | flops 2457600 | bytes 1638400 | tf_op jit(solution)/shard_map/concatenate | solution.py:77
  265.2 1.7 fusion.14
  (173 shorter events, 95.7 us)
Async XLA Ops:
  6.5 69.0 %all-gather.3.cloned.1.call-start = ((), (), s32[]{:S(2)}) async-start(), calls=%async_computation.2 | async-start | bytes 6144000 | tf_op jit(solution)/shard_map/all_gather | solution.py:11
  8.9 14.4 %copy-start.3 = (bf16[32,1,10,640]{3,0,2,1:T(8,128)(2,1)S(1)}, bf16[32,1,10,640]{3,0,2,1:T(8,128)(2,1)}, u32[]{:S(2)}) copy-start(bf16[32,1,10,640]{3,0,2,1:T(8,128)(2,1)} %param.8) | copy-start | bytes 1228804
  13.5 23.7 %all-to-all-start = ((bf16[32,2,3200]{2,1,0:T(2,128)(2,1)}), bf16[32,2,3200]{2,1,0:T(2,128)(2,1)}, u32[]{:S(2)}, u32[]{:S(2)}) async-start(bf16[32,2,3200]{2,1,0:T(2,128)(2,1)} %reshape.188), calls=%async_computation | async-start | bytes 819200 | tf_op jit(solution)/shard_map/all_to_all | solution.py:102
  23.3 118.5 %all-gather.5.cloned.1.call-start = ((), (), s32[]{:S(2)}) async-start(), calls=%async_computation.3 | async-start | bytes 10240000 | tf_op jit(solution)/shard_map/all_gather | solution.py:11
  49.1 23.8 %copy-start.1 = (bf16[1,1,320,640]{3,2,1,0:T(8,128)(2,1)S(1)}, bf16[1,1,320,640]{3,2,1,0:T(8,128)(2,1)}, u32[]{:S(2)}) copy-start(bf16[1,1,320,640]{3,2,1,0:T(8,128)(2,1)} %param.7) | copy-start | bytes 1228804
  141.8 106.7 %copy-start = (bf16[1,320,320]{2,1,0:T(8,128)(2,1)S(1)}, bf16[1,320,320]{2,1,0:T(8,128)(2,1)}, u32[]{:S(2)}) copy-start(bf16[1,320,320]{2,1,0:T(8,128)(2,1)} %param.9) | copy-start | bytes 614404
  252.8 12.4 %copy-start.2 = (bf16[1,1,320,640]{3,2,1,0:T(8,128)(2,1)S(1)}, bf16[1,1,320,640]{3,2,1,0:T(8,128)(2,1)}, u32[]{:S(2)}) copy-start(bf16[1,1,320,640]{3,2,1,0:T(8,128)(2,1)} %param.7) | copy-start | bytes 1228804
  252.8 12.4 %copy-start.4 = (bf16[1,320,320]{1,2,0:T(8,128)(2,1)S(1)}, bf16[1,320,320]{1,2,0:T(8,128)(2,1)}, u32[]{:S(2)}) copy-start(bf16[1,320,320]{1,2,0:T(8,128)(2,1)} %fusion.121) | copy-start | bytes 614404
  252.8 12.4 %copy-start.5 = (bf16[1,320,320]{1,2,0:T(8,128)(2,1)S(1)}, bf16[1,320,320]{1,2,0:T(8,128)(2,1)}, u32[]{:S(2)}) copy-start(bf16[1,320,320]{1,2,0:T(8,128)(2,1)} %get-tuple-element.83) | copy-start | bytes 614404
  252.8 12.4 %copy-start.6 = (bf16[1,320,320]{1,2,0:T(8,128)(2,1)S(1)}, bf16[1,320,320]{1,2,0:T(8,128)(2,1)}, u32[]{:S(2)}) copy-start(bf16[1,320,320]{1,2,0:T(8,128)(2,1)} %get-tuple-element.84) | copy-start | bytes 614404
Sparse Core Ops, SparseCore 0:
  9.8 60.2 all-gather.2
  73.0 68.7 all-gather.4
where the time goes:
time: 276 us; the launch traced here: 274 us
  waiting for transfers between devices  77.6 us (28%)
  matrix products  73.3 us (27%)
  local copies, waits for them, and re-layouts  53.8 us (19%)
  blocking collectives  22.9 us (8%)
  other arithmetic  20.8 us (8%)
  between operations  13.8 us (5%)
  starting transfers between devices  9.83 us (4%)
    all_gather x2, waiting for transfers between devices, entering(): gathered = jax.tree.map(lambda a: lax.all_gather(a, axis), part)  66.2 us
    dot_general x24, matrix products, transport(): jnp.einsum('nakb,cb->nakc', parts, link, preferred_element_type=jnp.float32)  32.4 us
    dot_general x24, matrix products, transport(): jnp.einsum('ab,nbc->nac', link, state, preferred_element_type=jnp.float32)  31.9 us
    dynamic_slice x46, local copies, waits for them, and re-layouts, one(): lax.dynamic_index_in_dim(a, lap, 0, False)  30.1 us
    all_to_all x1, blocking collectives, local(): lax.all_to_all(sigma_rows, 'energy', split_axis=0, concat_axis=2, tiled=T...  22.9 us
    concatenate x1, other arithmetic, sandwich(): jnp.concatenate([jnp.concatenate([state_re, state_im], -1), jnp.concatena...  12.3 us
    all_to_all x1, waiting for transfers between devices, local(): lax.all_to_all(g_lesser, 'energy', split_axis=2, concat_axis=0, tiled=True)  10.7 us
    all_to_all x1, starting transfers between devices, local(): lax.all_to_all(g_lesser, 'energy', split_axis=2, concat_axis=0, tiled=True)  9.79 us
  transfers between devices with their start and end apart: 3, of which 2 were waited for; matrix products, arithmetic and copies ran while one was open for 9% of the time, Pallas kernels for 0%

commit v1 on v0

v1 whole, which is shorter than its diff:
```python
import functools
import math

import jax
import jax.numpy as jnp
from jax import lax
from jax.experimental import pallas as pl
from jax.experimental.pallas import tpu as pltpu
from jax.sharding import PartitionSpec as P

MESH = pl.DeviceIdType.MESH
BF = jnp.bfloat16
F32 = jnp.float32
STARTS = (0, 2, 5, 8)
CHUNKS = 5


def spectral(owned, inter):
    count = owned.shape[0]
    half = owned.shape[-1] // 2
    rows = owned.shape[2]
    length = 2 * count
    freq = jnp.arange(length, dtype=jnp.int32)[:, None]
    point = jnp.arange(count, dtype=jnp.int32)[None, :]
    phase = (freq * point % length).astype(jnp.float32) * (2.0 * math.pi / length)
    fwd_re = jnp.cos(phase)
    fwd_im = -jnp.sin(phase)
    inv_re = jnp.cos(phase).T / length
    inv_im = jnp.sin(phase).T / length
    exact = lax.Precision.HIGHEST

    def forward(block):
        values = block.astype(jnp.float32)
        part_re = values[..., :half].reshape(count, -1)
        part_im = values[..., half:].reshape(count, -1)
        out_re = jnp.dot(fwd_re, part_re, precision=exact) - jnp.dot(
            fwd_im, part_im, precision=exact
        )
        out_im = jnp.dot(fwd_re, part_im, precision=exact) + jnp.dot(
            fwd_im, part_re, precision=exact
        )
        return (out_re, out_im)

    lesser_re, lesser_im = forward(owned)
    inter_re, inter_im = forward(inter)
    prod_re = lesser_re * inter_re - lesser_im * inter_im
    prod_im = lesser_re * inter_im + lesser_im * inter_re
    conv_re = jnp.dot(inv_re, prod_re, precision=exact) - jnp.dot(inv_im, prod_im, precision=exact)
    conv_im = jnp.dot(inv_re, prod_im, precision=exact) + jnp.dot(inv_im, prod_re, precision=exact)
    shape = (count, owned.shape[1], rows, half)
    return jnp.concatenate([-conv_im.reshape(shape), conv_re.reshape(shape)], axis=-1).astype(
        jnp.bfloat16
    )


def nn(a, b):
    return jnp.dot(a, b, preferred_element_type=F32)


def nt(a, b):
    return lax.dot_general(a, b, (((1,), (1,)), ((), ())), preferred_element_type=F32)


def one_of(value, options):
    hit = value == options[0]
    for option in options[1:]:
        hit = jnp.logical_or(hit, value == option)
    return hit


def remote(src, dst, sems, slot, slab):
    return pltpu.make_async_remote_copy(
        src_ref=src,
        dst_ref=dst,
        send_sem=sems.at[0, slot],
        recv_sem=sems.at[1, slot],
        device_id={"slab": slab},
        device_id_type=MESH,
    )


def scan_kernel(
    chips, sig_ref, link_ref, green_ref, out_ref,
    cbuf, abuf, pin, p1, p0, lin, lout, xin, xout, l1, l0, st, xb, sems,
):
    slab = lax.axis_index("slab")
    z = slab // 2
    c = slab % 2
    half = link_ref.shape[0]
    other = 2 * z + 1 - c
    up = slab + 2
    down = slab - 2
    has_up = z < chips - 1
    has_down = z > 0
    start = one_of(z, STARTS)
    end = one_of(z, tuple(s - 1 for s in STARTS[1:]) + (chips - 1,))
    carried = z >= STARTS[1]

    barrier = pltpu.get_barrier_semaphore()
    pl.semaphore_signal(barrier, inc=1, device_id={"slab": other}, device_id_type=MESH)

    @pl.when(has_up)
    def _():
        pl.semaphore_signal(barrier, inc=1, device_id={"slab": up}, device_id_type=MESH)

    @pl.when(has_down)
    def _():
        pl.semaphore_signal(barrier, inc=1, device_id={"slab": down}, device_id_type=MESH)

    pl.semaphore_wait(barrier, 1 + has_up.astype(jnp.int32) + has_down.astype(jnp.int32))

    send_c = remote(link_ref, cbuf.at[c], sems, 0, other)
    send_c.start()
    send_a = remote(sig_ref.at[1 - c], abuf.at[c], sems, 1, other)
    send_a.start()
    cbuf[c] = link_ref[...]
    abuf[c] = sig_ref[c]

    remote(link_ref, cbuf.at[1 - c], sems, 0, other).wait_recv()
    c0 = cbuf[0]
    c1 = cbuf[1]
    pair = nn(c1, c0).astype(BF)

    send_p = remote(p1, pin, sems, 2, up)

    @pl.when(start)
    def _():
        p1[...] = pair
        p0[...] = c0

    @pl.when(jnp.logical_not(start))
    def _():
        remote(p1, pin, sems, 2, up).wait_recv()
        p1[...] = nn(pair, pin[...]).astype(BF)
        p0[...] = nn(c0, pin[...]).astype(BF)

    @pl.when(jnp.logical_not(end))
    def _():
        send_p.start()

    remote(link_ref, abuf.at[1 - c], sems, 1, other).wait_recv()
    a0 = abuf[0]
    mid = nn(c1, a0).astype(BF)
    l1[...] = abuf[1].astype(F32) + nt(mid, c1)
    l0[...] = a0.astype(F32)

    send_l = remote(lout, lin, sems, 3, up)

    @pl.when(jnp.logical_not(start))
    def _():
        send_l.wait_recv()
        before = lin[...]
        l1[...] += nn(pair, nt(before, pair).astype(BF))

    @pl.when(jnp.logical_not(end))
    def _():
        lout[...] = l1[...].astype(BF)
        send_l.start()

    @pl.when(jnp.logical_not(start))
    def _():
        l0[...] += nn(c0, nt(lin[...], c0).astype(BF))

    depth = half // CHUNKS

    def carry(k, src):
        rows = pl.ds(k * depth, depth)
        return remote(src.at[rows, :], xin.at[rows, :], sems, 4 + k, up)

    @pl.when(carried)
    def _():
        for k in range(CHUNKS):
            carry(k, xin).wait_recv()

            @pl.when(jnp.logical_not(end))
            def _():
                carry(k, xin).start()

        before = xin[...]
        l1[...] += nn(p1[...], nt(before, p1[...]).astype(BF))

    @pl.when(jnp.logical_and(end, has_up))
    def _():
        xout[...] = l1[...].astype(BF)
        for k in range(CHUNKS):
            carry(k, xout).start()

    @pl.when(carried)
    def _():
        l0[...] += nn(p0[...], nt(xin[...], p0[...]).astype(BF))

    st[0] = l0[...].astype(BF)
    st[1] = l1[...].astype(BF)
    send_x = remote(st.at[1 - c], xb.at[c], sems, 4 + CHUNKS, other)
    send_x.start()
    xb[c] = st[c]

    green_re = green_ref[:, :half]
    green_im = green_ref[:, half:]

    remote(st.at[1 - c], xb.at[1 - c], sems, 4 + CHUNKS, other).wait_recv()
    x_re = xb[0]
    x_im = xb[1]
    left_re = (nn(green_re, x_re) - nn(green_im, x_im)).astype(BF)
    left_im = (nn(green_re, x_im) + nn(green_im, x_re)).astype(BF)
    cor_re = nt(left_re, green_re) + nt(left_im, green_im)
    cor_im = nt(left_im, green_re) - nt(left_re, green_im)
    out_ref[...] = jnp.concatenate([cor_re, cor_im], axis=1).astype(BF)

    send_c.wait_send()
    send_a.wait_send()
    send_x.wait_send()

    @pl.when(jnp.logical_not(end))
    def _():
        send_p.wait_send()
        send_l.wait_send()

    @pl.when(jnp.logical_or(jnp.logical_and(carried, has_up), end & has_up))
    def _():
        for k in range(CHUNKS):
            carry(k, xin).wait_send()


def scan(chips, sigma, link, green):
    half = link.shape[0]
    square = (half, half)
    vmem = pl.BlockSpec(memory_space=pltpu.VMEM)
    return pl.pallas_call(
        functools.partial(scan_kernel, chips),
        out_shape=jax.ShapeDtypeStruct((half, 2 * half), BF),
        in_specs=[vmem] * 3,
        out_specs=vmem,
        scratch_shapes=[
            pltpu.VMEM((2,) + square, BF),
            pltpu.VMEM((2,) + square, BF),
            pltpu.VMEM(square, BF),
            pltpu.VMEM(square, BF),
            pltpu.VMEM(square, BF),
            pltpu.VMEM(square, BF),
            pltpu.VMEM(square, BF),
            pltpu.VMEM(square, BF),
            pltpu.VMEM(square, BF),
            pltpu.VMEM(square, F32),
            pltpu.VMEM(square, F32),
            pltpu.VMEM((2,) + square, BF),
            pltpu.VMEM((2,) + square, BF),
            pltpu.SemaphoreType.DMA((2, 5 + CHUNKS)),
        ],
        compiler_params=pltpu.CompilerParams(
            collective_id=0, has_side_effects=True, vmem_limit_bytes=40 << 20
        ),
    )(sigma, link, green)


def solution(mesh):
    chips = mesh.shape["slab"] // 2

    def local(g_lesser, g_retarded, screened, coupling):
        owned = lax.all_to_all(g_lesser, "energy", split_axis=2, concat_axis=0, tiled=True)
        sigma_rows = spectral(owned, screened)
        sigma = lax.all_to_all(sigma_rows, "energy", split_axis=0, concat_axis=2, tiled=True)[0, 0]
        half = sigma.shape[-1] // 2
        streams = jnp.stack([sigma[:, :half], sigma[:, half:]])
        return scan(chips, streams, coupling[0], g_retarded[0, 0])[None, None]

    placed = (
        P("energy", "slab", None, None),
        P("energy", "slab", None, None),
        P(None, "slab", "energy", None),
        P("slab", None, None),
    )
    return jax.shard_map(
        local,
        mesh=mesh,
        in_specs=placed,
        out_specs=P("energy", "slab", None, None),
        check_vma=False,
    )
```

time: 276 us -> 125 us (0.45)
  waiting for transfers between devices: 77.6 us -> 10.5 us
  matrix products: 73.3 us -> 7.37 us
  Pallas kernels: 0 us -> 60.2 us
  local copies, waits for them, and re-layouts: 53.8 us -> 9.82 us
  other arithmetic: 20.8 us -> 3.42 us
  between operations: 13.8 us -> 0.27 us
    all_gather x2 -> x0, waiting for transfers between devices: 66.2 us -> none  [entering(): gathered = jax.tree.map(lambda a: lax.all_gather(a, axis), part)]
    dot_general x49 -> x0, matrix products: 66 us -> none  [the longest x24 32.4 us: transport(): jnp.einsum('nakb,cb->nakc', parts, link, preferred_element_type=jnp.float32)]
    pallas_call x0 -> x1, Pallas kernels: none -> 60.2 us  [scan(): pl.pallas_call(functools.partial(scan_kernel, chips), out_shape=jax.Shape...]
    dynamic_slice x46 -> x0, local copies, waits for them, and re-layouts: 30.1 us -> none  [one(): lax.dynamic_index_in_dim(a, lap, 0, False)]
    concatenate x1 -> x0, other arithmetic: 12.3 us -> none  [sandwich(): jnp.concatenate([jnp.concatenate([state_re, state_im], -1), jnp.concatena...]
    another operation x24 -> x1, local copies, waits for them, and re-layouts: 9.74 us -> 0.13 us  [local(): streams = jnp.stack([sigma[:, :half], sigma[:, half:]])]
    convert_element_type x24 -> x0, other arithmetic: 3.01 us -> none  [the longest x23 2.17 us: compose(): (transport(link_two, state_one) + state_two.astype(jnp.float32)).astype(j...]
    unnamed x18 -> x11, local copies, waits for them, and re-layouts: 5.87 us -> 4.97 us
  transfers between devices with their start and end apart: 3 -> 1, of which waited for: 2 -> 1; matrix products, arithmetic and copies ran while one was open for 9% -> 3% of each run, Pallas kernels for 0% -> 0%
where the time goes in v1:
time: 125 us; the launch traced here: 124 us
  Pallas kernels  60.2 us (48%)
  blocking collectives  23 us (18%)
  waiting for transfers between devices  10.5 us (8%)
  starting transfers between devices  9.85 us (8%)
  local copies, waits for them, and re-layouts  9.82 us (8%)
  matrix products  7.37 us (6%)
  other arithmetic  3.42 us (3%)
    pallas_call x1, Pallas kernels, scan(): pl.pallas_call(functools.partial(scan_kernel, chips), out_shape=jax.Shape...  60.2 us
    all_to_all x1, blocking collectives, local(): lax.all_to_all(sigma_rows, 'energy', split_axis=0, concat_axis=2, tiled=T...  23 us
    all_to_all x1, waiting for transfers between devices, local(): lax.all_to_all(g_lesser, 'energy', split_axis=2, concat_axis=0, tiled=True)  10.5 us
    all_to_all x1, starting transfers between devices, local(): lax.all_to_all(g_lesser, 'energy', split_axis=2, concat_axis=0, tiled=True)  9.85 us
    unnamed x11, local copies, waits for them, and re-layouts  4.97 us
    unnamed x1, other arithmetic  3.11 us
  transfers between devices with their start and end apart: 1, of which 1 were waited for; matrix products, arithmetic and copies ran while one was open for 3% of the time, Pallas kernels for 0%

profile of v1, /device:TPU:705, one launch (start us, length us, event | category | flops | bytes accessed | tf_op | source)
XLA Modules:
  0.0 124.4 jit_solution(3914752449213929980)
XLA Ops:
  0.0 1.6 %copy.13 = bf16[1,1,320,640]{3,1,0,2:T(2,128)(2,1)S(1)} copy(bf16[1,1,320,640]{3,2,1,0:T(8,128)(2,1)} %param.4) | data formatting | bytes 819200 | tf_op args[0]
  1.6 0.5 broadcast.79
  2.2 3.1 %reduce.2 = bf16[320,640]{1,0:T(8,128)(2,1)S(1)} reduce(bf16[320,1,1,640]{3,2,1,0:T(2,128)(2,1)S(1)} %bitcast.37, bf16[]{:T(256)} %broadcast.79), dimensions={1,2}, to_apply=%bitcast.33.reduce_sub_computation | reduce | bytes 819202
  5.3 0.9 reshape.68
  6.2 9.8 %all-to-all-start = ((bf16[32,2,3200]{2,1,0:T(2,128)(2,1)}), bf16[32,2,3200]{2,1,0:T(2,128)(2,1)S(1)}, u32[]{:S(2)}, u32[]{:S(2)}) async-start(bf16[32,2,3200]{2,1,0:T(2,128)(2,1)} %reshape.68), calls=%async_computation | async-start | bytes 819200 | tf_op jit(solution)/shard_map/all_to_all | solution.py:260
  16.3 0.2 reshape.65
  16.5 0.6 fusion.21
  17.2 0.2 reshape.66
  17.5 0.6 fusion.17
  18.1 0.6 convolution_add_fusion.1
  18.7 0.6 convolution_subtract_fusion
  19.3 10.5 %all-to-all-done = bf16[32,2,3200]{2,1,0:T(2,128)(2,1)S(1)} async-done(((bf16[32,2,3200]{2,1,0:T(2,128)(2,1)}), bf16[32,2,3200]{2,1,0:T(2,128)(2,1)S(1)}, u32[]{:S(2)}, u32[]{:S(2)}) %all-to-all-start) | async-done | bytes 409632 | tf_op jit(solution)/shard_map/all_to_all | solution.py:260
  29.8 0.3 reshape.69
  30.2 2.4 %bitcast_reduce_fusion = bf16[320,640]{1,0:T(8,128)(2,1)S(1)} fusion(bf16[320,1,1,640]{3,2,1,0:T(2,128)(2,1)S(1)} %reshape.69), kind=kLoop, calls=%fused_computation.101 | loop fusion | bytes 819200 | tf_op jit(solution)/shard_map/all_to_all | solution.py:260
  32.7 0.2 fusion.90
  32.9 0.2 reshape.63
  33.1 0.2 reshape.64
  33.3 0.6 fusion.19
  33.9 0.6 fusion.23
  34.5 0.6 convolution_subtract_fusion.1
  35.2 0.8 multiply_add_fusion
  36.0 0.6 fusion.29
  36.6 0.6 fusion.28
  37.2 0.6 fusion.1
  37.8 0.6 fusion.2
  38.4 0.3 concatenate.17
  38.7 0.3 concatenate.16
  39.1 0.2 maximum_bitcast_fusion
  39.3 23.0 %all_to_all.21 = bf16[32,1,10,640]{3,2,1,0:T(8,128)(2,1)S(1)} all-to-all(bf16[32,1,10,640]{3,2,1,0:T(8,128)(2,1)S(1)} %maximum_bitcast_fusion), channel_id=1, replica_groups=mesh['energy'=32,'slab'=24] {'energy'}, dimensions={0} | all-to-all | bytes 819200 | tf_op jit(solution)/shard_map/all_to_all | solution.py:262
  62.7 0.7 copy-done
  63.5 60.2 %shard_map.46 = bf16[320,640]{1,0:T(8,128)(2,1)S(1)} custom-call(bf16[2,320,320]{2,1,0:T(8,128)(2,1)S(1)} %pad_maximum_fusion.sig_ref, bf16[320,320]{1,0:T(8,128)(2,1)S(1)} %bitcast.36, bf16[320,640]{1,0:T(8,128)(2,1)S(1)} %bitcast.35), custom_call_target="tpu_custom_call" | custom-call | tf_op jit(solution)/shard_map/pallas_call | solution.py:229
  123.7 0.8 copy.15
  (12 shorter events, 0.9 us)
Async XLA Ops:
  5.3 10.8 %copy-start.2 = (bf16[32,1,10,640]{3,0,2,1:T(8,128)(2,1)S(1)}, bf16[32,1,10,640]{3,0,2,1:T(8,128)(2,1)}, u32[]{:S(2)}) copy-start(bf16[32,1,10,640]{3,0,2,1:T(8,128)(2,1)} %param.6) | copy-start | bytes 1228804
  6.2 23.6 %all-to-all-start = ((bf16[32,2,3200]{2,1,0:T(2,128)(2,1)}), bf16[32,2,3200]{2,1,0:T(2,128)(2,1)S(1)}, u32[]{:S(2)}, u32[]{:S(2)}) async-start(bf16[32,2,3200]{2,1,0:T(2,128)(2,1)} %reshape.68), calls=%async_computation | async-start | bytes 819200 | tf_op jit(solution)/shard_map/all_to_all | solution.py:260
  62.4 1.0 copy-start
  62.4 1.1 copy-start.1
